TPU v7x, 512 devices: a whole 4x4x16 slice. The times are simulated.
512 devices in a mesh: pair: 64 (over z, y), virt: 8 (over x, core).
Axes of the slice: x: 4, y: 4, z: 16, core: 2. Of those that a mesh axis runs over, the one named last changes fastest.
Arguments:
- amplitudes: bfloat16 [512, 8, 4096], P('pair', 'virt'), may hold values from -6 to 6
- partner: int32 [512], P('pair'), may hold values from 0 to 511, as said below
- integrals: bfloat16 [64, 4096, 4096], P('virt', 'pair'), may hold values from -0.09375 to 0.09375
- pattern: int32 [64], P('virt'), may hold values from 0 to 15, as said below
- owner: int32 [16], replicated, may hold values from 0 to 15, as said below
Outputs:
- ladder: bfloat16 [512, 16, 4096], P('pair', 'virt')
Inputs may be any that keep to these rules, and one draw needn't show every extreme that they name: partner pairs each pair with another one and is its own inverse; the partner of a pair held by index j of pair is held by index j + 64 / 2 modulo 64, that is half the pair axis away. `pattern`: every ab tile pair appears exactly four times in all. owner names every ab tile pair exactly once.
All inputs are finite; a program needn't handle non-finite values.
Results may differ from a plain program's by a relative error of at most 0.0051.
Values may be sent and summed in bfloat16 or wider, within the bound.
A program may use at most 64 MiB of HBM per device.

v0:
```python
import jax
import jax.numpy as jnp
from jax import lax
from jax.sharding import PartitionSpec as P

TILE = 64


def from_partner(value, axis, stride):
    mask = 2**stride
    pairs = [(source, source ^ mask) for source in range(lax.axis_size(axis))]
    return lax.ppermute(value, axis, pairs)


def symmetrize(plain, mirrored):
    count, width = (plain.shape[0], plain.shape[1])
    flipped = jnp.swapaxes(mirrored.reshape(count, width, TILE, TILE), 2, 3).reshape(plain.shape)
    return (plain.astype(jnp.float32) + flipped.astype(jnp.float32)).astype(jnp.bfloat16)


def shards(amplitudes, partner, integrals, pattern, owner):
    rows = amplitudes.shape[0]
    top_bit = lax.axis_size("pair").bit_length() - 2
    other = from_partner(amplitudes, "pair", top_bit)
    symmetric = symmetrize(amplitudes, jnp.take(other, partner % rows, axis=0))
    piece = lax.all_gather(symmetric, "pair", axis=0, tiled=True)
    flat = piece.reshape(piece.shape[0], -1)
    terms = jnp.einsum("rc,kjc->rkj", flat, integrals, preferred_element_type=jnp.float32)
    selector = (owner[None, :] == pattern[:, None]).astype(jnp.float32)
    spread = jnp.einsum("pkj,ks->psj", terms, selector, precision=lax.Precision.HIGHEST)
    routed = lax.all_to_all(spread, "pair", split_axis=0, concat_axis=2, tiled=True)
    summed = lax.psum_scatter(routed, "virt", scatter_dimension=1, tiled=True)
    result = summed.astype(jnp.bfloat16)
    return result


def solution(mesh):
    return jax.shard_map(
        shards,
        mesh=mesh,
        in_specs=(P("pair", "virt", None), P("pair"), P("virt", "pair", None), P("virt"), P()),
        out_specs=P("pair", "virt", None),
        check_vma=False,
    )
```

profile of v0, /device:TPU:8, one launch (start us, length us, event | category | flops | bytes accessed | tf_op | source)
XLA Modules:
  0.0 357.5 jit_solution(16470699635944835072)
XLA Ops:
  6.5 0.0 all-gather.2.cloned.1.call-start
  6.5 15.7 %collective-permute-start = (bf16[8,1,4096]{2,0,1:T(8,128)(2,1)}, bf16[8,1,4096]{2,0,1:T(8,128)(2,1)S(1)}, u32[]{:S(2)}, u32[]{:S(2)}) collective-permute-start(bf16[8,1,4096]{2,0,1:T(8,128)(2,1)} %param.5), channel_id=1, source_target_pairs={{0,256},{8,264},{16,272},{24,280},{32,288},{40,296},{48,304},{56,3... | collective-permute-start | bytes 196616 | tf_op jit(solution)/shard_map/ppermute | solution.py:12
  22.3 0.7 compare_and_fusion
  22.9 3.8 %collective-permute-done = bf16[8,1,4096]{2,0,1:T(8,128)(2,1)S(1)} collective-permute-done((bf16[8,1,4096]{2,0,1:T(8,128)(2,1)}, bf16[8,1,4096]{2,0,1:T(8,128)(2,1)S(1)}, u32[]{:S(2)}, u32[]{:S(2)}) %collective-permute-start) | collective-permute-done | bytes 65568 | tf_op jit(solution)/shard_map/ppermute | solution.py:12
  26.8 0.6 gather_fusion
  27.4 0.2 gather.7
  27.5 0.1 copy.21
  27.7 0.1 convert_bitcast_fusion
  27.8 0.1 reshape.45
  27.9 1.5 add_convert_fusion
  29.4 0.0 all-gather.2.cloned.1.call-update
  29.4 0.0 copy-start
  29.4 0.0 copy-start.1
  29.4 0.0 reduce-scatter.2.cloned.1.call-start
  29.5 146.3 %all-gather.2.cloned.1.call-done = bf16[512,1,4096]{2,0,1:T(8,128)(2,1)} async-done(((bf16[8,1,4096]{2,0,1:T(8,128)(2,1)}), bf16[512,1,4096]{2,0,1:T(8,128)(2,1)}) %all-gather.2.cloned.1.call-update) | async-done | bytes 4194320 | tf_op jit(solution)/shard_map/all_gather | solution.py:26
  175.8 6.3 %fusion = f32[512,8,64]{0,1,2:T(8,128)S(1)} fusion(bf16[512,1,4096]{2,0,1:T(8,128)(2,1)} %all-gather.2.cloned.1.call-done, bf16[8,64,4096]{2,1,0:T(8,128)(2,1)} %param.7), kind=kOutput, calls=%fused_computation.1 | convolution fusion | flops 2147483648 | bytes 9437184 | tf_op jit(solution)/shard_map/rc,kjc->rkj/dot_general | solution.py:28
  182.1 0.0 copy-done
  182.1 0.0 copy-done.1
  182.1 1.1 convolution_bitcast_fusion
  183.2 4.2 %copy.23 = f32[512,16,64]{2,1,0:T(8,128)} copy(f32[512,16,64]{0,1,2:T(8,128)S(1)} %convolution_bitcast_fusion) | data formatting | bytes 4194304 | tf_op jit(solution)/shard_map/pkj,ks->psj/transpose | solution.py:30
  187.4 4.6 %reshape.61 = f32[64,1,8192]{2,1,0:T(1,128)S(1)} reshape(f32[512,16,64]{2,1,0:T(8,128)} %copy.23) | data formatting | bytes 4194304
  192.0 101.3 %all_to_all.18 = f32[64,1,8192]{2,1,0:T(1,128)} all-to-all(f32[64,1,8192]{2,1,0:T(1,128)S(1)} %reshape.61), channel_id=1, replica_groups=mesh['pair'=64,'virt'=8] {'pair'}, dimensions={0} | all-to-all | bytes 4194304 | tf_op jit(solution)/shard_map/all_to_all | solution.py:31
  293.3 0.5 broadcast.45
  293.8 7.5 %reduce = f32[64,8192]{1,0:T(8,128)S(1)} reduce(f32[64,1,8192]{2,1,0:T(1,128)} %all_to_all.18, f32[]{:T(128)} %broadcast.45), dimensions={1}, to_apply=%all_to_all.13.reduce_sub_computation | reduce | bytes 4194308 | tf_op jit(solution)/shard_map/all_to_all | solution.py:31
  301.3 3.0 reshape.62
  304.4 6.6 %copy.27 = f32[8,16,64,64]{3,2,0,1:T(8,128)} copy(f32[8,16,64,64]{3,1,0,2:T(8,128)} %bitcast.24) | data formatting | bytes 4194304 | tf_op jit(solution)/shard_map/all_to_all | solution.py:31
  310.9 4.8 %reshape.60 = f32[8,16,4096]{2,0,1:T(8,128)} reshape(f32[8,16,64,64]{3,2,0,1:T(8,128)} %copy.27) | data formatting | bytes 4194304 | tf_op jit(solution)/shard_map/all_to_all | solution.py:31
  315.7 0.0 reduce-scatter.2.cloned.1.call-update
  315.7 33.2 %reduce-scatter.2.cloned.1.call-done = f32[8,2,4096]{2,0,1:T(8,128)} async-done(((f32[8,16,4096]{2,0,1:T(8,128)}), f32[8,2,4096]{2,0,1:T(8,128)}) %reduce-scatter.2.cloned.1.call-update) | async-done | bytes 262160 | tf_op jit(solution)/shard_map/reduce_scatter | solution.py:32
  348.9 1.0 convert_element_type.32
  349.9 0.8 copy.26
  (1 shorter events, 0.0 us)
Async XLA Ops:
  6.5 169.3 %all-gather.2.cloned.1.call-start = ((), (), s32[]{:S(2)}) async-start(), calls=%async_computation.2 | async-start | bytes 4259840 | tf_op jit(solution)/shard_map/all_gather | solution.py:26
  6.5 20.2 %collective-permute-start = (bf16[8,1,4096]{2,0,1:T(8,128)(2,1)}, bf16[8,1,4096]{2,0,1:T(8,128)(2,1)S(1)}, u32[]{:S(2)}, u32[]{:S(2)}) collective-permute-start(bf16[8,1,4096]{2,0,1:T(8,128)(2,1)} %param.5), channel_id=1, source_target_pairs={{0,256},{8,264},{16,272},{24,280},{32,288},{40,296},{48,304},{56,3... | collective-permute-start | bytes 196616 | tf_op jit(solution)/shard_map/ppermute | solution.py:12
  29.4 152.7 %copy-start = (s32[16]{0:T(128)S(1)}, s32[16]{0:T(128)}, u32[]{:S(2)}) copy-start(s32[16]{0:T(128)} %param.9) | copy-start | bytes 196
  29.4 152.7 %copy-start.1 = (s32[8]{0:T(128)S(1)}, s32[8]{0:T(128)}, u32[]{:S(2)}) copy-start(s32[8]{0:T(128)} %param.8) | copy-start | bytes 100
  29.4 319.5 %reduce-scatter.2.cloned.1.call-start = ((), (), s32[]{:S(2)}) async-start(), calls=%async_computation.3 | async-start | bytes 2359296 | tf_op jit(solution)/shard_map/reduce_scatter | solution.py:32
Sparse Core Ops, SparseCore 0:
  29.5 146.2 all-gather.1
  315.8 33.0 reduce-scatter.1
where the time goes:
time: 358 us
  waiting for transfers between devices  183 us (51%)
  blocking collectives  101 us (28%)
  local copies, waits for them, and re-layouts  25.4 us (7%)
  starting transfers between devices  15.8 us (4%)
  between operations  13.5 us (4%)
  other arithmetic  10.7 us (3%)
  matrix products  7.4 us (2%)
    all_gather x1, waiting for transfers between devices, shards(): piece = lax.all_gather(symmetric, 'pair', axis=0, tiled=True)  146 us
    all_to_all x1, blocking collectives, shards(): lax.all_to_all(spread, 'pair', split_axis=0, concat_axis=2, tiled=True)  101 us
    reduce_scatter x1, waiting for transfers between devices, shards(): summed = lax.psum_scatter(routed, 'virt', scatter_dimension=1, tiled=True)  33.2 us
    ppermute x1, starting transfers between devices, from_partner(): return lax.ppermute(value, axis, pairs)  15.7 us
    all_to_all x3, local copies, waits for them, and re-layouts, shards(): lax.all_to_all(spread, 'pair', split_axis=0, concat_axis=2, tiled=True)  11.8 us
    unnamed x6, local copies, waits for them, and re-layouts  7.61 us
    all_to_all x1, other arithmetic, shards(): lax.all_to_all(spread, 'pair', split_axis=0, concat_axis=2, tiled=True)  7.54 us
  transfers between devices with their start and end apart: 3, of which 3 were waited for; matrix products, arithmetic and copies ran while one was open for 0% of the time, Pallas kernels for 0%

commit v1 on v0

--- a/solution.py
+++ b/solution.py
@@ -19,11 +19,18 @@
 
 
 def shards(amplitudes, partner, integrals, pattern, owner):
+
+    def bring_numbers(values, mesh_name):
+        later = lax.axis_size(mesh_name)
+        q_next = jnp.stack(later * [values])
+        n_now = lax.all_to_all(q_next, mesh_name, 0, 0)
+        return jnp.concatenate(n_now, axis=0)
+
     rows = amplitudes.shape[0]
     top_bit = lax.axis_size("pair").bit_length() - 2
     other = from_partner(amplitudes, "pair", top_bit)
     symmetric = symmetrize(amplitudes, jnp.take(other, partner % rows, axis=0))
-    piece = lax.all_gather(symmetric, "pair", axis=0, tiled=True)
+    piece = bring_numbers(symmetric, "pair")
     flat = piece.reshape(piece.shape[0], -1)
     terms = jnp.einsum("rc,kjc->rkj", flat, integrals, preferred_element_type=jnp.float32)
     selector = (owner[None, :] == pattern[:, None]).astype(jnp.float32)

time: 358 us -> 413 us (1.15)
  blocking collectives: 101 us -> 306 us
  waiting for transfers between devices: 183 us -> 37.1 us
    all_to_all x0 -> x1, blocking collectives: none -> 203 us  [bring_numbers(): n_now = lax.all_to_all(q_next, mesh_name, 0, 0)]
    all_gather x1 -> x0, waiting for transfers between devices: 146 us -> none  [shards(): piece = lax.all_gather(symmetric, 'pair', axis=0, tiled=True)]
  transfers between devices with their start and end apart: 3 -> 2, of which waited for: 3 -> 2; matrix products, arithmetic and copies ran while one was open for 0% -> 0% of each run, Pallas kernels for 0% -> 0%
where the time goes in v1:
time: 413 us; the launch traced here: 412 us
  blocking collectives  306 us (74%)
  waiting for transfers between devices  37.1 us (9%)
  local copies, waits for them, and re-layouts  25.9 us (6%)
  starting transfers between devices  15.7 us (4%)
  between operations  13.5 us (3%)
  other arithmetic  10.1 us (2%)
    all_to_all x1, blocking collectives, bring_numbers(): n_now = lax.all_to_all(q_next, mesh_name, 0, 0)  203 us
    all_to_all x1, blocking collectives, shards(): lax.all_to_all(spread, 'pair', split_axis=0, concat_axis=2, tiled=True)  103 us
    reduce_scatter x1, waiting for transfers between devices, shards(): summed = lax.psum_scatter(routed, 'virt', scatter_dimension=1, tiled=True)  33.2 us
    ppermute x1, starting transfers between devices, from_partner(): return lax.ppermute(value, axis, pairs)  15.7 us
    all_to_all x3, local copies, waits for them, and re-layouts, shards(): lax.all_to_all(spread, 'pair', split_axis=0, concat_axis=2, tiled=True)  11.8 us
  transfers between devices with their start and end apart: 2, of which 2 were waited for; matrix products, arithmetic and copies ran while one was open for 0% of the time, Pallas kernels for 0%

profile of v1, /device:TPU:8, one launch (start us, length us, event | category | flops | bytes accessed | tf_op | source)
XLA Modules:
  0.0 412.3 jit_solution(597661854694317441)
XLA Ops:
  6.5 0.0 reduce-scatter.2.cloned.1.call-start
  6.5 15.7 %collective-permute-start = (bf16[8,1,4096]{2,0,1:T(8,128)(2,1)}, bf16[8,1,4096]{2,0,1:T(8,128)(2,1)S(1)}, u32[]{:S(2)}, u32[]{:S(2)}) collective-permute-start(bf16[8,1,4096]{2,0,1:T(8,128)(2,1)} %param.5), channel_id=1, source_target_pairs={{0,256},{8,264},{16,272},{24,280},{32,288},{40,296},{48,304},{56,3... | collective-permute-start | bytes 196616 | tf_op jit(solution)/shard_map/ppermute | solution.py:12
  22.3 0.7 compare_and_fusion
  22.9 3.8 collective-permute-done
  26.8 0.6 gather_fusion
  27.4 0.2 gather.7
  27.5 0.1 convert_bitcast_fusion
  27.6 0.1 copy.21
  27.8 0.1 reshape.44
  27.9 0.9 fusion.3
  28.8 0.5 stack.2
  29.3 0.0 copy-start.2
  29.3 202.8 %all_to_all.23 = bf16[64,8,1,4096]{3,1,2,0:T(8,128)(2,1)S(1)} all-to-all(bf16[64,8,1,4096]{3,1,2,0:T(8,128)(2,1)S(1)} %stack.2), channel_id=1, replica_groups=mesh['pair'=64,'virt'=8] {'pair'}, dimensions={0} | all-to-all | bytes 8388608 | tf_op jit(solution)/shard_map/all_to_all | solution.py:26
  232.1 0.0 copy-done.2
  232.1 0.0 copy-start
  232.1 0.0 copy-start.1
  232.1 2.8 fusion
  234.9 0.0 copy-done
  235.0 0.0 copy-done.1
  235.0 1.1 convolution_bitcast_fusion
  236.1 4.2 %copy.23 = f32[512,16,64]{2,1,0:T(8,128)} copy(f32[512,16,64]{0,1,2:T(8,128)S(1)} %convolution_bitcast_fusion) | data formatting | bytes 4194304 | tf_op jit(solution)/shard_map/pkj,ks->psj/transpose | solution.py:37
  240.2 4.6 %reshape.60 = f32[64,1,8192]{2,1,0:T(1,128)S(1)} reshape(f32[512,16,64]{2,1,0:T(8,128)} %copy.23) | data formatting | bytes 4194304
  244.8 103.2 %all_to_all.24 = f32[64,1,8192]{2,1,0:T(1,128)} all-to-all(f32[64,1,8192]{2,1,0:T(1,128)S(1)} %reshape.60), channel_id=1, replica_groups=mesh['pair'=64,'virt'=8] {'pair'}, dimensions={0} | all-to-all | bytes 4194304 | tf_op jit(solution)/shard_map/all_to_all | solution.py:38
  348.0 0.5 broadcast.48
  348.6 7.5 %reduce = f32[64,8192]{1,0:T(8,128)S(1)} reduce(f32[64,1,8192]{2,1,0:T(1,128)} %all_to_all.24, f32[]{:T(128)} %broadcast.48), dimensions={1}, to_apply=%all_to_all.17.reduce_sub_computation | reduce | bytes 4194308 | tf_op jit(solution)/shard_map/all_to_all | solution.py:38
  356.1 3.1 reshape.61
  359.2 6.5 %copy.27 = f32[8,16,64,64]{3,2,0,1:T(8,128)} copy(f32[8,16,64,64]{3,1,0,2:T(8,128)} %bitcast.27) | data formatting | bytes 4194304 | tf_op jit(solution)/shard_map/all_to_all | solution.py:38
  365.7 4.8 %reshape.59 = f32[8,16,4096]{2,0,1:T(8,128)} reshape(f32[8,16,64,64]{3,2,0,1:T(8,128)} %copy.27) | data formatting | bytes 4194304 | tf_op jit(solution)/shard_map/all_to_all | solution.py:38
  370.5 0.0 reduce-scatter.2.cloned.1.call-update
  370.5 33.2 %reduce-scatter.2.cloned.1.call-done = f32[8,2,4096]{2,0,1:T(8,128)} async-done(((f32[8,16,4096]{2,0,1:T(8,128)}), f32[8,2,4096]{2,0,1:T(8,128)}) %reduce-scatter.2.cloned.1.call-update) | async-done | bytes 262160 | tf_op jit(solution)/shard_map/reduce_scatter | solution.py:39
  403.7 1.0 convert_element_type.35
  404.7 0.8 copy.26
  (1 shorter events, 0.0 us)
Async XLA Ops:
  6.5 397.2 %reduce-scatter.2.cloned.1.call-start = ((), (), s32[]{:S(2)}) async-start(), calls=%async_computation.3 | async-start | bytes 2359296 | tf_op jit(solution)/shard_map/reduce_scatter | solution.py:39
  6.5 20.2 %collective-permute-start = (bf16[8,1,4096]{2,0,1:T(8,128)(2,1)}, bf16[8,1,4096]{2,0,1:T(8,128)(2,1)S(1)}, u32[]{:S(2)}, u32[]{:S(2)}) collective-permute-start(bf16[8,1,4096]{2,0,1:T(8,128)(2,1)} %param.5), channel_id=1, source_target_pairs={{0,256},{8,264},{16,272},{24,280},{32,288},{40,296},{48,304},{56,3... | collective-permute-start | bytes 196616 | tf_op jit(solution)/shard_map/ppermute | solution.py:12
  29.3 202.8 %copy-start.2 = (bf16[8,64,4096]{2,1,0:T(8,128)(2,1)S(1)}, bf16[8,64,4096]{2,1,0:T(8,128)(2,1)}, u32[]{:S(2)}) copy-start(bf16[8,64,4096]{2,1,0:T(8,128)(2,1)} %param.7) | copy-start | bytes 12582916
  232.1 2.9 copy-start
  232.1 2.9 copy-start.1
Sparse Core Ops, SparseCore 0:
  370.6 33.0 reduce-scatter.1
